TPU v7x, 32 devices: a whole 2x2x4 slice. The times are simulated.
32 devices in a mesh: team: 2 (over core), obs: 4 (over z), grid: 4 (over y, x).
Axes of the slice: x: 2, y: 2, z: 4, core: 2. Of those that a mesh axis runs over, the one named last changes fastest.
Arguments:
- design_panel: bfloat16 [8192, 1024], P('obs', ('team', 'grid')), may hold values from -6 to 6
- design_front: bfloat16 [8192, 6144], P('obs', 'grid'), may hold values from -6 to 6
- arc_ids: int32 [8192], P('obs'), may hold values from 0 to 127
- arc_weight: float32 [128], replicated, may hold values from 0.5 to 2
- row_counts: int32 [4], P('obs'), may hold values from 128 to 2048, as said below
- panel_inverse: float32 [1024, 1024], P(('team', 'obs')), may hold values from -6.525546e-05 to 0.0020539933
- front: float32 [6144, 6144], P(('team', 'obs'), 'grid'), may hold values from -1.2 to 21.2
Outputs:
- factor_row: float32 [1024, 6144], P(('team', 'obs'), 'grid')
- front_next: float32 [6144, 6144], P(('team', 'obs'), 'grid')
Inputs may be any that keep to these rules, and one draw needn't show every extreme that they name: `row_counts`: every count is a multiple of 128, and in every draw some shard's count equals 2048.
All inputs are finite; a program needn't handle non-finite values.
Results may differ from a plain program's by a relative error of at most 0.0035.
Values may be sent and summed in bfloat16 or wider, within the bound.
A program may use at most 64 MiB of HBM per device.

v0:
```python
import jax
import jax.numpy as jnp
from jax import lax
from jax.sharding import PartitionSpec as P


def from_root(value, axis, source):
    kept = jnp.where(lax.axis_index(axis) == source, value, 0).astype(value.dtype)
    return lax.psum(kept, axis)


def live_weights(arc_ids, arc_weight, row_counts):
    row_total = arc_ids.shape[0]
    arc_total = arc_weight.shape[0]
    onehot = (
        arc_ids[:, None] == lax.broadcasted_iota(jnp.int32, (row_total, arc_total), 1)
    ).astype(jnp.float32)
    looked = jnp.dot(
        onehot, arc_weight, precision=lax.Precision.HIGHEST, preferred_element_type=jnp.float32
    )
    is_live = lax.broadcasted_iota(jnp.int32, (row_total,), 0) < row_counts[0]
    return looked * is_live.astype(jnp.float32)


def contract_rows(panel_rows, scaled_rows):
    return lax.dot_general(
        panel_rows, scaled_rows, (((0,), (0,)), ((), ())), preferred_element_type=jnp.float32
    )


def whole_factor(panel_inverse, block_whole):
    return jnp.dot(
        lax.all_gather(panel_inverse, ("team", "obs"), axis=0, tiled=True),
        block_whole,
        precision=lax.Precision.HIGHEST,
        preferred_element_type=jnp.float32,
    )


def local(design_panel, design_front, arc_ids, arc_weight, row_counts, panel_inverse, front):
    weights = live_weights(arc_ids, arc_weight, row_counts)
    scaled_front = (design_front.astype(jnp.float32) * weights[:, None]).astype(jnp.bfloat16)
    front_cols = design_front.shape[1]
    live_blocks = (row_counts[0] + 255) // 256
    panel_piece = lax.all_gather(design_panel, "grid", axis=1, tiled=True)

    def add_block(block_index, running):
        row_start = block_index * 256
        panel_rows = lax.dynamic_slice_in_dim(panel_piece, row_start, 256, 0)
        scaled_rows = lax.dynamic_slice_in_dim(scaled_front, row_start, 256, 0)
        return running + contract_rows(panel_rows, scaled_rows)

    partial_value = lax.fori_loop(
        0, live_blocks, add_block, jnp.zeros((panel_piece.shape[1], front_cols), jnp.float32)
    )
    slab_rows = panel_inverse.shape[0]
    place_index = lax.axis_index(("team", "obs"))
    block_part = lax.psum_scatter(partial_value, "obs", scatter_dimension=0, tiled=True)
    block_whole = lax.all_gather(block_part, ("team", "obs"), axis=0, tiled=True)
    factor_cols = whole_factor(panel_inverse, block_whole)
    factor_part = lax.dynamic_slice_in_dim(factor_cols, place_index * slab_rows, slab_rows, 0)
    tile_rows = front.shape[0]
    tile_ratio = factor_cols.shape[1] // tile_rows
    offset = place_index % tile_ratio * tile_rows
    own_slice = lax.dynamic_slice_in_dim(factor_cols, offset, tile_rows, 1)
    factor_rows = from_root(
        own_slice.astype(jnp.bfloat16), "grid", place_index // tile_ratio
    ).astype(own_slice.dtype)
    update = lax.dot_general(
        factor_rows,
        factor_cols,
        (((0,), (0,)), ((), ())),
        precision=lax.Precision.HIGHEST,
        preferred_element_type=jnp.float32,
    )
    return (factor_part, front - update)


def solution(mesh):
    placed = (
        P("obs", ("team", "grid")),
        P("obs", "grid"),
        P("obs"),
        P(),
        P("obs"),
        P(("team", "obs"), None),
        P(("team", "obs"), "grid"),
    )
    return jax.shard_map(
        local,
        mesh=mesh,
        in_specs=placed,
        out_specs=(P(("team", "obs"), "grid"), P(("team", "obs"), "grid")),
        check_vma=False,
    )
```

profile of v0, /device:TPU:20, one launch (start us, length us, event | category | flops | bytes accessed | tf_op | source)
XLA Modules:
  0.0 348.4 jit_solution(14501843023129149956)
XLA Ops:
  8.0 0.0 copy-start
  8.0 0.0 all-gather.4.cloned.1.call-start
  8.1 0.7 all-gather.4.cloned.1.call-update
  8.7 0.0 reduce-scatter.2.cloned.1.call-start
  9.5 0.0 copy-done
  9.5 1.4 fusion.5
  10.9 6.5 %multiply_convert_fusion = bf16[2048,1536]{1,0:T(8,128)(2,1)} fusion(bf16[2048,1536]{1,0:T(8,128)(2,1)} %param.10, f32[2048]{0:T(1024)S(1)} %fusion.7), kind=kLoop, calls=%fused_computation.4 | loop fusion | flops 9437184 | bytes 12591104 | tf_op jit(solution)/shard_map/convert_element_type | solution.py:42
  17.4 29.3 %all-gather.4.cloned.1.call-done = bf16[2048,512]{1,0:T(8,128)(2,1)} async-done(((bf16[2048,128]{1,0:T(8,128)(2,1)}), bf16[2048,512]{1,0:T(8,128)(2,1)}) %all-gather.4.cloned.1.call-update) | async-done | bytes 2097168 | tf_op jit(solution)/shard_map/all_gather | solution.py:45
  46.7 0.4 broadcast_in_dim.9
  47.1 7.9 %while.10 = (s32[]{:T(128)}, f32[512,1536]{1,0:T(8,128)S(1)}, s32[]{:T(128)}, bf16[2048,512]{1,0:T(8,128)(2,1)}, bf16[2048,1536]{1,0:T(8,128)(2,1)}, /*index=5*/s32[]{:T(128)}, s32[]{:T(128)}, s32[]{:T(128)}, s32[]{:T(128)}) while((s32[]{:T(128)}, f32[512,1536]{1,0:T(8,128)S(1)}, s32[]{:T(128)}, bf16[2048,512]{1,0:T(8,128)(2,1)}, ...), condition=%wide.region_1.2_spmd, body=%wide.region_0.1_spmd.sunk | while | flops 403439616 | bytes 7341195 | solution.py:53
  47.1 1.9 convolution_add_fusion.2
  49.1 1.9 convolution_add_fusion.2
  51.1 1.9 convolution_add_fusion.2
  53.0 1.9 convolution_add_fusion.2
  55.0 0.0 copy-start.1
  55.0 1.7 copy-done.1
  56.6 0.0 reduce-scatter.2.cloned.1.call-update
  56.7 0.0 all-gather.8.cloned.1.call-start
  56.7 0.5 all-gather.8.cloned.1.call-update
  57.2 0.0 all-gather.6.cloned.1.call-start
  57.3 87.8 %reduce-scatter.2.cloned.1.call-done = f32[128,1536]{1,0:T(8,128)} async-done(((f32[512,1536]{1,0:T(8,128)}), f32[128,1536]{1,0:T(8,128)}) %reduce-scatter.2.cloned.1.call-update) | async-done | bytes 786448 | tf_op jit(solution)/shard_map/reduce_scatter | solution.py:58
  145.1 0.0 all-gather.6.cloned.1.call-update
  145.1 0.0 all-reduce.2.cloned.1.call-start
  145.2 11.0 %all-gather.8.cloned.1.call-done = f32[1024,1024]{1,0:T(8,128)} async-done(((f32[128,1024]{1,0:T(8,128)}), f32[1024,1024]{1,0:T(8,128)}) %all-gather.8.cloned.1.call-update) | async-done | bytes 4194320 | tf_op jit(solution)/shard_map/all_gather | solution.py:33
  156.2 64.7 %all-gather.6.cloned.1.call-done = f32[1024,1536]{1,0:T(8,128)} async-done(((f32[128,1536]{1,0:T(8,128)}), f32[1024,1536]{1,0:T(8,128)}) %all-gather.6.cloned.1.call-update) | async-done | bytes 6291472 | tf_op jit(solution)/shard_map/all_gather | solution.py:59
  220.9 43.1 %fusion.9 = f32[1536,1024]{1,0:T(8,128)S(1)} fusion(f32[1024,1536]{1,0:T(8,128)} %all-gather.6.cloned.1.call-done, f32[1024,1024]{1,0:T(8,128)} %all-gather.8.cloned.1.call-done), kind=kOutput, calls=%fused_computation.16 | convolution fusion | flops 19327352832 | bytes 16777216 | tf_op jit(solution)/shard_map/dot_general | solution.py:32
  264.0 0.0 copy-start.2
  264.0 2.6 copy-done.2
  266.6 1.6 fusion.4
  268.2 0.0 all-reduce.2.cloned.1.call-update
  268.2 1.2 dynamic-slice_bitcast_fusion
  269.4 1.1 copy.9
  270.6 58.4 %all-reduce.2.cloned.1.call-done = bf16[1024,768]{0,1:T(8,128)(2,1)} async-done(((bf16[1024,768]{0,1:T(8,128)(2,1)}), bf16[1024,768]{0,1:T(8,128)(2,1)}) %all-reduce.2.cloned.1.call-update) | async-done | bytes 1572880 | tf_op jit(solution)/shard_map/psum | solution.py:9
  329.0 12.3 %convolution_subtract_fusion = f32[768,1536]{1,0:T(8,128)} fusion(f32[768,1536]{1,0:T(8,128)} %param.15, bf16[1024,768]{0,1:T(8,128)(2,1)} %all-reduce.2.cloned.1.call-done, f32[1536,1024]{1,0:T(8,128)} %copy-done.2), kind=kOutput, calls=%fused_computation.5 | convolution fusion | flops 14496694272 | bytes 17301504 | tf_op jit(solution)/shard_map/dot_general | solution.py:69
  (1 shorter events, 0.0 us)
Async XLA Ops:
  8.0 1.5 copy-start
  8.0 38.7 %all-gather.4.cloned.1.call-start = ((), (), s32[]{:S(2)}) async-start(), calls=%async_computation.1 | async-start | bytes 2621440 | tf_op jit(solution)/shard_map/all_gather | solution.py:45
  8.7 136.3 %reduce-scatter.2.cloned.1.call-start = ((), (), s32[]{:S(2)}) async-start(), calls=%async_computation.2 | async-start | bytes 3932160 | tf_op jit(solution)/shard_map/reduce_scatter | solution.py:58
  55.0 1.7 copy-start.1
  56.7 99.5 %all-gather.8.cloned.1.call-start = ((), (), s32[]{:S(2)}) async-start(), calls=%async_computation.4 | async-start | bytes 4718592 | tf_op jit(solution)/shard_map/all_gather | solution.py:33
  57.2 163.6 %all-gather.6.cloned.1.call-start = ((), (), s32[]{:S(2)}) async-start(), calls=%async_computation.3 | async-start | bytes 7077888 | tf_op jit(solution)/shard_map/all_gather | solution.py:59
  145.1 183.9 %all-reduce.2.cloned.1.call-start = ((), (), s32[]{:S(2)}) async-start(), calls=%async_computation.5 | async-start | bytes 3145728 | tf_op jit(solution)/shard_map/psum | solution.py:9
  264.0 2.6 copy-start.2
Sparse Core Ops, SparseCore 0:
  10.6 36.0 all-gather.3
  56.8 88.2 reduce-scatter.1
  268.3 60.6 all-reduce.1
Sparse Core Ops, SparseCore 1:
  58.7 97.4 all-gather.7
  157.6 63.2 all-gather.5
where the time goes:
time: 352 us; the launch traced here: 348 us
  waiting for transfers between devices  252 us (72%)
  matrix products  64.5 us (18%)
  between operations  16 us (5%)
  other arithmetic  8.11 us (2%)
  local copies, waits for them, and re-layouts  7.01 us (2%)
    reduce_scatter x1, waiting for transfers between devices, local(): lax.psum_scatter(partial_value, 'obs', scatter_dimension=0, tiled=True)  87.8 us
    all_gather x1, waiting for transfers between devices, local(): lax.all_gather(block_part, ('team', 'obs'), axis=0, tiled=True)  64.7 us
    psum x1, waiting for transfers between devices, from_root(): return lax.psum(kept, axis)  58.4 us
    dot_general x1, matrix products, whole_factor(): jnp.dot(lax.all_gather(panel_inverse, ('team', 'obs'), axis=0, tiled=True...  43.1 us
    all_gather x1, waiting for transfers between devices, local(): panel_piece = lax.all_gather(design_panel, 'grid', axis=1, tiled=True)  29.3 us
    dot_general x1, matrix products, local(): lax.dot_general(factor_rows, factor_cols, (((0,), (0,)), ((), ())), preci...  12.3 us
    all_gather x1, waiting for transfers between devices, whole_factor(): lax.all_gather(panel_inverse, ('team', 'obs'), axis=0, tiled=True)  11 us
    dot_general x4, matrix products, contract_rows(): lax.dot_general(panel_rows, scaled_rows, (((0,), (0,)), ((), ())), prefer...  7.73 us
  transfers between devices with their start and end apart: 5, of which 5 were waited for; matrix products, arithmetic and copies ran while one was open for 3% of the time, Pallas kernels for 0%

commit v1 on v0

v1 whole, which is shorter than its diff:
```python
import jax
import jax.numpy as jnp
from jax import lax
from jax.sharding import PartitionSpec as P


def live_weights(arc_ids, arc_weight, row_counts):
    row_total = arc_ids.shape[0]
    arc_total = arc_weight.shape[0]
    hit = arc_ids[:, None] == lax.broadcasted_iota(jnp.int32, (row_total, arc_total), 1)
    looked = jnp.sum(jnp.where(hit, arc_weight[None, :], 0.0), axis=1)
    is_live = lax.broadcasted_iota(jnp.int32, (row_total,), 0) < row_counts[0]
    return looked * is_live.astype(jnp.float32)


def contract_rows(left, right):
    return lax.dot_general(
        left, right, (((0,), (0,)), ((), ())), preferred_element_type=jnp.float32
    )


def local(design_panel, design_front, arc_ids, arc_weight, row_counts, panel_inverse, front):
    high = lax.reduce_precision(panel_inverse, 8, 7)
    split = jnp.concatenate([high, panel_inverse - high], axis=1).astype(jnp.bfloat16)
    inverse_whole = lax.all_gather(split, ("team", "obs"), axis=0, tiled=True)
    weights = live_weights(arc_ids, arc_weight, row_counts)
    scaled_front = (design_front.astype(jnp.float32) * weights[:, None]).astype(jnp.bfloat16)
    panel_piece = lax.all_gather(design_panel, "grid", axis=1, tiled=True)
    partial_value = contract_rows(panel_piece, scaled_front)
    slab_rows = panel_inverse.shape[0]
    place_index = lax.axis_index(("team", "obs"))
    block_part = lax.psum_scatter(partial_value, "obs", scatter_dimension=0, tiled=True)
    block_part = block_part.astype(jnp.bfloat16)
    block_whole = lax.all_gather(block_part, ("team", "obs"), axis=0, tiled=True)
    factor_cols = jnp.dot(
        inverse_whole,
        jnp.concatenate([block_whole, block_whole], axis=0),
        preferred_element_type=jnp.float32,
    )
    factor_part = lax.dynamic_slice_in_dim(factor_cols, place_index * slab_rows, slab_rows, 0)
    factor_cols = factor_cols.astype(jnp.bfloat16)
    tile_rows = front.shape[0]
    tile_ratio = factor_cols.shape[1] // tile_rows
    offset = place_index % tile_ratio * tile_rows
    own_slice = lax.dynamic_slice_in_dim(factor_cols, offset, tile_rows, 1)
    kept = jnp.where(lax.axis_index("grid") == place_index // tile_ratio, own_slice, 0)
    factor_rows = lax.psum(kept.astype(jnp.bfloat16), "grid")
    return (factor_part, front - contract_rows(factor_rows, factor_cols))


def solution(mesh):
    placed = (
        P("obs", ("team", "grid")),
        P("obs", "grid"),
        P("obs"),
        P(),
        P("obs"),
        P(("team", "obs"), None),
        P(("team", "obs"), "grid"),
    )
    return jax.shard_map(
        local,
        mesh=mesh,
        in_specs=placed,
        out_specs=(P(("team", "obs"), "grid"), P(("team", "obs"), "grid")),
        check_vma=False,
    )
```

time: 352 us -> 279 us (0.79)
  matrix products: 64.5 us -> 27 us
  waiting for transfers between devices: 252 us -> 226 us
  local copies, waits for them, and re-layouts: 7.01 us -> 2.08 us
    dot_general x7 -> x3, matrix products: 64.5 us -> 27 us  [the longest x2 15.1 us: contract_rows(): lax.dot_general(left, right, (((0,), (0,)), ((), ())), preferred_element_...]
    all_gather x1, waiting for transfers between devices: 64.7 us -> 39.3 us  [local(): lax.all_gather(block_part, ('team', 'obs'), axis=0, tiled=True)]
    all_gather x1, waiting for transfers between devices: 29.3 us -> 35.9 us  [local(): panel_piece = lax.all_gather(design_panel, 'grid', axis=1, tiled=True)]
    reduce_scatter x1, waiting for transfers between devices: 87.8 us -> 82.2 us  [local(): lax.psum_scatter(partial_value, 'obs', scatter_dimension=0, tiled=True)]
    unnamed x7 -> x2, local copies, waits for them, and re-layouts: 5.46 us -> 0.01 us
    convert_element_type x1, other arithmetic: 6.52 us -> 1.92 us  [local(): block_part = block_part.astype(jnp.bfloat16)]
  transfers between devices with their start and end apart: 5 -> 5, of which waited for: 5 -> 5; matrix products, arithmetic and copies ran while one was open for 3% -> 2% of each run, Pallas kernels for 0% -> 0%
where the time goes in v1:
time: 279 us; the launch traced here: 277 us
  waiting for transfers between devices  226 us (81%)
  matrix products  27 us (10%)
  between operations  15.9 us (6%)
  other arithmetic  5.59 us (2%)
    reduce_scatter x1, waiting for transfers between devices, local(): lax.psum_scatter(partial_value, 'obs', scatter_dimension=0, tiled=True)  82.2 us
    psum x1, waiting for transfers between devices, local(): factor_rows = lax.psum(kept.astype(jnp.bfloat16), 'grid')  58.7 us
    all_gather x1, waiting for transfers between devices, local(): lax.all_gather(block_part, ('team', 'obs'), axis=0, tiled=True)  39.3 us
    all_gather x1, waiting for transfers between devices, local(): panel_piece = lax.all_gather(design_panel, 'grid', axis=1, tiled=True)  35.9 us
    dot_general x2, matrix products, contract_rows(): lax.dot_general(left, right, (((0,), (0,)), ((), ())), preferred_element_...  15.1 us
    dot_general x1, matrix products, local(): jnp.dot(inverse_whole, jnp.concatenate([block_whole, block_whole], axis=0...  11.9 us
    all_gather x1, waiting for transfers between devices, local(): inverse_whole = lax.all_gather(split, ('team', 'obs'), axis=0, tiled=True)  9.1 us
  transfers between devices with their start and end apart: 5, of which 5 were waited for; matrix products, arithmetic and copies ran while one was open for 2% of the time, Pallas kernels for 0%

profile of v1, /device:TPU:20, one launch (start us, length us, event | category | flops | bytes accessed | tf_op | source)
XLA Modules:
  0.0 276.8 jit_solution(38822958594479527)
XLA Ops:
  8.0 0.0 all-gather.6.cloned.1.call-start
  8.0 0.7 all-gather.6.cloned.1.call-update
  8.7 0.0 reduce-scatter.2.cloned.1.call-start
  9.4 1.3 select_reduce_fusion
  10.8 0.0 copy-start
  10.8 35.9 %all-gather.6.cloned.1.call-done = bf16[2048,512]{1,0:T(8,128)(2,1)} async-done(((bf16[2048,128]{1,0:T(8,128)(2,1)}), bf16[2048,512]{1,0:T(8,128)(2,1)}) %all-gather.6.cloned.1.call-update) | async-done | bytes 2097168 | tf_op jit(solution)/shard_map/all_gather | solution.py:28
  46.7 8.7 %fusion.6 = f32[512,1536]{0,1:T(8,128)} fusion(bf16[2048,512]{1,0:T(8,128)(2,1)} %all-gather.6.cloned.1.call-done, bf16[2048,1536]{1,0:T(8,128)(2,1)} %param.8, f32[2048]{0:T(1024)S(1)} %fusion.8), kind=kOutput, calls=%fused_computation.8 | convolution fusion | flops 3230662656 | bytes 11542528 | tf_op jit(solution)/shard_map/dot_general | solution.py:17
  55.4 0.0 reduce-scatter.2.cloned.1.call-update
  55.4 0.0 all-gather.4.cloned.1.call-start
  55.4 0.0 copy-done
  55.5 0.1 reduce-precision_convert_fusion
  55.5 0.8 pad_maximum_fusion
  56.4 0.0 all-gather.4.cloned.1.call-update
  56.4 0.0 all-gather.8.cloned.1.call-start
  56.5 82.2 %reduce-scatter.2.cloned.1.call-done = f32[128,1536]{0,1:T(8,128)} async-done(((f32[512,1536]{0,1:T(8,128)}), f32[128,1536]{0,1:T(8,128)}) %reduce-scatter.2.cloned.1.call-update) | async-done | bytes 786448 | tf_op jit(solution)/shard_map/reduce_scatter | solution.py:32
  138.7 1.9 convert_element_type.18
  140.6 0.0 all-gather.8.cloned.1.call-update
  140.6 0.0 all-reduce.2.cloned.1.call-start
  140.7 9.1 %all-gather.4.cloned.1.call-done = bf16[1024,2048]{1,0:T(8,128)(2,1)} async-done(((bf16[128,2048]{1,0:T(8,128)(2,1)}), bf16[1024,2048]{1,0:T(8,128)(2,1)}) %all-gather.4.cloned.1.call-update) | async-done | bytes 4194320 | tf_op jit(solution)/shard_map/all_gather | solution.py:25
  149.8 39.3 %all-gather.8.cloned.1.call-done = bf16[1024,1536]{0,1:T(8,128)(2,1)} async-done(((bf16[128,1536]{0,1:T(8,128)(2,1)}), bf16[1024,1536]{0,1:T(8,128)(2,1)}) %all-gather.8.cloned.1.call-update) | async-done | bytes 3145744 | tf_op jit(solution)/shard_map/all_gather | solution.py:34
  189.1 11.9 %fusion.10 = (bf16[1024,1536]{1,0:T(8,128)(2,1)S(1)}, f32[1024,1536]{1,0:T(8,128)}) fusion(bf16[1024,2048]{1,0:T(8,128)(2,1)} %all-gather.4.cloned.1.call-done, bf16[1024,1536]{0,1:T(8,128)(2,1)} %all-gather.8.cloned.1.call-done), kind=kOutput, calls=%fused_computation.20 | convolution fusion | flops 6456606720 | bytes 16777216 | tf_op jit(solution)/shard_map/dot_general | solution.py:35
  201.1 1.4 dynamic-slice_select_fusion
  202.5 0.0 all-reduce.2.cloned.1.call-update
  202.5 2.1 constant_dynamic-slice_fusion
  204.6 58.7 %all-reduce.2.cloned.1.call-done = bf16[1024,768]{1,0:T(8,128)(2,1)} async-done(((bf16[1024,768]{1,0:T(8,128)(2,1)}), bf16[1024,768]{1,0:T(8,128)(2,1)}) %all-reduce.2.cloned.1.call-update) | async-done | bytes 1572880 | tf_op jit(solution)/shard_map/psum | solution.py:47
  263.3 6.4 %convolution_subtract_fusion = f32[768,1536]{1,0:T(8,128)} fusion(f32[768,1536]{1,0:T(8,128)} %param.13, bf16[1024,768]{1,0:T(8,128)(2,1)} %all-reduce.2.cloned.1.call-done, bf16[1024,1536]{1,0:T(8,128)(2,1)S(1)} %get-tuple-element.4), kind=kOutput, calls=%fused_computation.7 | convolution fusion | flops 2417098752 | bytes 14155776 | tf_op jit(solution)/shard_map/dot_general | solution.py:17
  (1 shorter events, 0.0 us)
Async XLA Ops:
  8.0 38.7 %all-gather.6.cloned.1.call-start = ((), (), s32[]{:S(2)}) async-start(), calls=%async_computation.2 | async-start | bytes 2621440 | tf_op jit(solution)/shard_map/all_gather | solution.py:28
  8.7 130.0 %reduce-scatter.2.cloned.1.call-start = ((), (), s32[]{:S(2)}) async-start(), calls=%async_computation.3 | async-start | bytes 3932160 | tf_op jit(solution)/shard_map/reduce_scatter | solution.py:32
  10.8 44.7 %copy-start = (f32[128,1024]{1,0:T(8,128)S(1)}, f32[128,1024]{1,0:T(8,128)}, u32[]{:S(2)}) copy-start(f32[128,1024]{1,0:T(8,128)} %param.12) | copy-start | bytes 1572868
  55.4 94.4 %all-gather.4.cloned.1.call-start = ((), (), s32[]{:S(2)}) async-start(), calls=%async_computation.1 | async-start | bytes 4718592 | tf_op jit(solution)/shard_map/all_gather | solution.py:25
  56.4 132.7 %all-gather.8.cloned.1.call-start = ((), (), s32[]{:S(2)}) async-start(), calls=%async_computation.4 | async-start | bytes 3538944 | tf_op jit(solution)/shard_map/all_gather | solution.py:34
  140.6 122.7 %all-reduce.2.cloned.1.call-start = ((), (), s32[]{:S(2)}) async-start(), calls=%async_computation.5 | async-start | bytes 3145728 | tf_op jit(solution)/shard_map/psum | solution.py:47
Sparse Core Ops, SparseCore 0:
  10.6 36.0 all-gather.5
  55.5 83.1 reduce-scatter.1
  202.6 60.6 all-reduce.1
Sparse Core Ops, SparseCore 1:
  58.1 91.7 all-gather.3
  151.8 37.2 all-gather.7

commit v2 on v1

--- a/solution.py
+++ b/solution.py
@@ -1,6 +1,10 @@
+import functools
+
 import jax
 import jax.numpy as jnp
 from jax import lax
+from jax.experimental import pallas as pl
+from jax.experimental.pallas import tpu as pltpu
 from jax.sharding import PartitionSpec as P
 
 
@@ -48,6 +52,342 @@
     return (factor_part, front - contract_rows(factor_rows, factor_cols))
 
 
+MESH = pl.DeviceIdType.MESH
+
+
+def exchange(
+    ratio, panel, front_cols, weights, inverse_rows,
+    blk, tile, inv,
+    panels, scaled, outgoing, incoming, own_sum,
+    local_sem, panel_send, panel_recv, sum_send, sum_recv,
+    line_send, line_recv, inv_send, inv_recv,
+    team_send, team_recv, team_inv_send, team_inv_recv, tile_send, tile_recv,
+):
+    team, z, grid = lax.axis_index("team"), lax.axis_index("obs"), lax.axis_index("grid")
+    lines = blk.shape[2]
+    groups = blk.shape[1]
+    x, y = lax.rem(grid, 2), lax.div(grid, 2)
+    beside_x = y * 2 + (1 - x)
+    beside_y = (1 - y) * 2 + x
+    across = (1 - y) * 2 + (1 - x)
+    partner = 1 - team
+    place = team * lines + z
+    root, half = lax.div(place, ratio), lax.rem(place, ratio)
+    per_half = lines // ratio
+    root_x, root_y = lax.rem(root, 2), lax.div(root, 2)
+    is_root = grid == root
+    is_relay = grid == root_y * 2 + (1 - root_x)
+    width = panel.shape[1]
+    piece = scaled.shape[2]
+
+    barrier = pltpu.get_barrier_semaphore()
+    for peer in (beside_x, beside_y, across):
+        pl.semaphore_signal(barrier, inc=1, device_id={"grid": peer}, device_id_type=MESH)
+    for p in range(1, lines):
+        pl.semaphore_signal(
+            barrier, inc=1, device_id={"obs": lax.rem(z + p, lines)}, device_id_type=MESH
+        )
+    pl.semaphore_signal(barrier, inc=1, device_id={"team": partner}, device_id_type=MESH)
+    pl.semaphore_wait(barrier, lines + 3)
+
+    def remote(src, dst, send, recv, where):
+        return pltpu.make_async_remote_copy(
+            src_ref=src, dst_ref=dst, send_sem=send, recv_sem=recv,
+            device_id=where, device_id_type=MESH,
+        )
+
+    def panel_slot(index):
+        return panels.at[lax.div(index, 2), :, pl.ds(pl.multiple_of(lax.rem(index, 2) * width, width), width)]
+
+    panel_copies = []
+    for k, peer in enumerate((beside_x, beside_y, across)):
+        panel_copies.append(
+            remote(panel, panel_slot(grid), panel_send.at[k], panel_recv.at[k], {"grid": peer})
+        )
+        panel_copies[-1].start()
+    own_panel = pltpu.make_async_copy(panel, panel_slot(grid), local_sem.at[0])
+    own_panel.start()
+    own_inv = pltpu.make_async_copy(inverse_rows, inv.at[team, z], local_sem.at[1])
+    own_inv.start()
+
+    def line_sends(ref_of, send, recv, s):
+        for d, step in ((0, 1), (1, -1)):
+            held = z - step * s
+            ok = (held >= 0) & (held < lines) & (z + step >= 0) & (z + step < lines)
+            idx = jnp.clip(held, 0, lines - 1)
+            nxt = jnp.clip(z + step, 0, lines - 1)
+
+            @pl.when(ok)
+            def _():
+                remote(ref_of(idx), ref_of(idx), send.at[d, s], recv.at[d, s], {"obs": nxt}).start()
+
+    def line_waits(ref_of, send, recv, s, then):
+        for d, step in ((0, 1), (1, -1)):
+            came = z - step * (s + 1)
+
+            @pl.when((came >= 0) & (came < lines))
+            def _():
+                idx = jnp.clip(came, 0, lines - 1)
+                pltpu.make_async_copy(ref_of(idx), ref_of(idx), recv.at[d, s]).wait()
+                then(idx)
+
+    def line_drain(ref_of, send):
+        for s in range(lines - 1):
+            for d, step in ((0, 1), (1, -1)):
+                held = z - step * s
+
+                @pl.when((held >= 0) & (held < lines) & (z + step >= 0) & (z + step < lines))
+                def _():
+                    idx = jnp.clip(held, 0, lines - 1)
+                    pltpu.make_async_copy(ref_of(idx), ref_of(idx), send.at[d, s]).wait()
+
+    def inv_of(idx):
+        return inv.at[team, idx]
+
+    def inv_to_team(idx):
+        remote(inv.at[team, idx], inv.at[team, idx], team_inv_send.at[idx],
+               team_inv_recv.at[idx], {"team": partner}).start()
+
+    own_inv.wait()
+    line_sends(inv_of, inv_send, inv_recv, 0)
+    inv_to_team(z)
+
+    rows = panel.shape[0]
+    step_rows = 256
+
+    @pl.loop(0, rows // step_rows)
+    def _(i):
+        at = pl.ds(pl.multiple_of(i * step_rows, step_rows), step_rows)
+        factor = weights[at, :]
+        for q in range(lines):
+            part = front_cols[at, q * piece:(q + 1) * piece].astype(jnp.float32)
+            scaled[q, at, :] = (part * factor).astype(jnp.bfloat16)
+
+    own_panel.wait()
+    sum_copies = []
+    for order in range(groups):
+        g = y if order == 0 else 1 - y
+        if order == 0:
+            panel_copies[0].wait_recv()
+        else:
+            panel_copies[1].wait_recv()
+            panel_copies[2].wait_recv()
+            for s in range(lines - 2):
+                line_waits(inv_of, inv_send, inv_recv, s, inv_to_team)
+                line_sends(inv_of, inv_send, inv_recv, s + 1)
+        for p in (2, 1, 3, 0):
+            dest = lax.rem(z + p, lines)
+            total = contract_rows(panels[g], scaled[dest])
+            if p == 0:
+                own_sum[order] = total
+            else:
+                outgoing[order, p - 1] = total.astype(jnp.bfloat16)
+                copy = remote(
+                    outgoing.at[order, p - 1], incoming.at[order, p - 1],
+                    sum_send.at[order, p - 1], sum_recv.at[order, p - 1], {"obs": dest},
+                )
+                copy.start()
+                sum_copies.append(copy)
+
+    line_waits(inv_of, inv_send, inv_recv, lines - 2, inv_to_team)
+
+    def finished(t, g, order, idx):
+        @pl.when(is_root & (lax.div(idx, per_half) == half))
+        def _():
+            q = lax.rem(idx, per_half)
+            for k, peer in ((0, beside_x), (1, beside_y)):
+                remote(blk.at[t, g, idx], tile.at[t, g, q], tile_send.at[k, t, g, q],
+                       tile_recv.at[t, g, q], {"grid": peer}).start()
+            pltpu.make_async_copy(blk.at[t, g, idx], tile.at[t, g, q], tile_recv.at[t, g, q]).start()
+
+    def line_done(g, order, idx):
+        remote(blk.at[team, g, idx], blk.at[team, g, idx], team_send.at[g, idx],
+               team_recv.at[g, idx], {"team": partner}).start()
+        finished(team, g, order, idx)
+
+    for order in range(groups):
+        g = y if order == 0 else 1 - y
+        total = own_sum[order]
+        for p in (1, 3, 2):
+            sum_copies[order * (lines - 1) + (2, 1, 3).index(p)].wait_recv()
+            total = total + incoming[order, p - 1].astype(jnp.float32)
+        blk[team, g, z] = total.astype(jnp.bfloat16)
+
+        def of(idx, g=g):
+            return blk.at[team, g, idx]
+
+        line_sends(of, line_send.at[order], line_recv.at[order], 0)
+        line_done(g, order, z)
+
+    for s in range(lines - 1):
+        for order in range(groups):
+            g = y if order == 0 else 1 - y
+
+            def of(idx, g=g):
+                return blk.at[team, g, idx]
+
+            line_waits(of, line_send.at[order], line_recv.at[order], s,
+                       lambda idx: line_done(g, order, idx))
+            if s + 1 < lines - 1:
+                line_sends(of, line_send.at[order], line_recv.at[order], s + 1)
+
+    for order in range(groups):
+        g = y if order == 0 else 1 - y
+        for idx in range(lines):
+            pltpu.make_async_copy(
+                blk.at[partner, g, idx], blk.at[partner, g, idx], team_recv.at[g, idx]
+            ).wait()
+            finished(partner, g, order, idx)
+
+    for t in (team, partner):
+        for order in range(groups):
+            g = y if order == 0 else 1 - y
+            for q in range(per_half):
+                dst = tile.at[t, g, q]
+                pltpu.make_async_copy(dst, dst, tile_recv.at[t, g, q]).wait()
+
+                @pl.when(is_relay)
+                def _():
+                    remote(dst, dst, tile_send.at[0, t, g, q], tile_recv.at[t, g, q],
+                           {"grid": beside_y}).start()
+
+    for copy in panel_copies + sum_copies:
+        copy.wait_send()
+    line_drain(inv_of, inv_send)
+    for order in range(groups):
+        g = y if order == 0 else 1 - y
+        line_drain(lambda idx: blk.at[team, g, idx], line_send.at[order])
+    for idx in range(lines):
+        ref = inv.at[team, idx]
+        pltpu.make_async_copy(ref, ref, team_inv_send.at[idx]).wait()
+        ref = inv.at[partner, idx]
+        pltpu.make_async_copy(ref, ref, team_inv_recv.at[idx]).wait()
+        for g in range(groups):
+            ref = blk.at[team, g, idx]
+            pltpu.make_async_copy(ref, ref, team_send.at[g, idx]).wait()
+    for t in range(2):
+        for g in range(groups):
+            for q in range(per_half):
+                ref = tile.at[t, g, q]
+
+                @pl.when(is_root | is_relay)
+                def _():
+                    pltpu.make_async_copy(ref, ref, tile_send.at[0, t, g, q]).wait()
+
+                @pl.when(is_root)
+                def _():
+                    pltpu.make_async_copy(ref, ref, tile_send.at[1, t, g, q]).wait()
+
+
+def finish(spot, blk, tile, inv, front, factor_out, front_out, cols, high, low):
+    pieces, blocks, size = blk.shape[1], blk.shape[0], blk.shape[2]
+    piece = blk.shape[3]
+    whole = blocks * size
+    slab = factor_out.shape[0]
+
+    def factor_of(source, q, r):
+        total = inv[r * size:(r + 1) * size, whole:whole + 1].astype(jnp.float32)
+        total = total * source[r, q].astype(jnp.float32)
+        for k in range(r + 1):
+            total += jnp.dot(
+                inv[r * size:(r + 1) * size, k * size:(k + 1) * size], source[k, q],
+                preferred_element_type=jnp.float32,
+            )
+        return total
+
+    for r in range(blocks):
+        for q in range(pieces):
+            value = factor_of(blk, q, r)
+            cols[q, r * size:(r + 1) * size, :] = value.astype(jnp.bfloat16)
+            for part in range(size // slab):
+                @pl.when(spot[0] == r * (size // slab) + part)
+                def _():
+                    factor_out[:, q * piece:(q + 1) * piece] = value[part * slab:(part + 1) * slab]
+        for q in range(tile.shape[1]):
+            value = factor_of(tile, q, r)
+            top = value.astype(jnp.bfloat16)
+            high[q, r * size:(r + 1) * size, :] = top
+            low[q, r * size:(r + 1) * size, :] = (value - top.astype(jnp.float32)).astype(jnp.bfloat16)
+
+    for h in range(tile.shape[1]):
+        for q in range(pieces):
+            update = contract_rows(high[h], cols[q]) + contract_rows(low[h], cols[q])
+            at = (slice(h * piece, (h + 1) * piece), slice(q * piece, (q + 1) * piece))
+            front_out[at] = front[at] - update
+
+
+def local_kernels(lines, design_panel, design_front, arc_ids, arc_weight, row_counts, panel_inverse, front):
+    bf16 = jnp.bfloat16
+    weights = live_weights(arc_ids, arc_weight, row_counts)[:, None]
+    slab, whole = panel_inverse.shape
+    rows, width = design_panel.shape
+    cols = design_front.shape[1]
+    tile_rows = front.shape[0]
+    ratio = cols // tile_rows
+    piece = cols // lines
+    groups = 2
+    size = 2 * width
+    place = lax.axis_index(("team", "obs"))
+    top = lax.reduce_precision(panel_inverse, 8, 7)
+    row_at = lax.broadcasted_iota(jnp.int32, (slab, whole), 0) + place * slab
+    on_diagonal = lax.broadcasted_iota(jnp.int32, (slab, whole), 1) == row_at
+    rest = jnp.sum(jnp.where(on_diagonal, panel_inverse - top, 0.0), axis=1, keepdims=True)
+    inverse_rows = jnp.concatenate(
+        [top, jnp.broadcast_to(rest, (slab, 128))], axis=1
+    ).astype(bf16)
+    vmem = pl.BlockSpec(memory_space=pltpu.VMEM)
+    dma = pltpu.SemaphoreType.DMA
+    hops = lines - 1
+    halves = lines // ratio
+    blk, tile, inv = pl.pallas_call(
+        functools.partial(exchange, ratio),
+        out_shape=(
+            jax.ShapeDtypeStruct((2, groups, lines, size, piece), bf16),
+            jax.ShapeDtypeStruct((2, groups, halves, size, piece), bf16),
+            jax.ShapeDtypeStruct((2, lines) + inverse_rows.shape, bf16),
+        ),
+        in_specs=[vmem] * 4,
+        out_specs=(vmem,) * 3,
+        scratch_shapes=[
+            pltpu.VMEM((groups, rows, size), bf16),
+            pltpu.VMEM((lines, rows, piece), bf16),
+            pltpu.VMEM((groups, hops, size, piece), bf16),
+            pltpu.VMEM((groups, hops, size, piece), bf16),
+            pltpu.VMEM((groups, size, piece), jnp.float32),
+            dma((2,)), dma((3,)), dma((3,)),
+            dma((groups, hops)), dma((groups, hops)),
+            dma((groups, 2, hops)), dma((groups, 2, hops)),
+            dma((2, hops)), dma((2, hops)),
+            dma((groups, lines)), dma((groups, lines)),
+            dma((lines,)), dma((lines,)),
+            dma((2, 2, groups, halves)), dma((2, groups, halves)),
+        ],
+        compiler_params=pltpu.CompilerParams(
+            collective_id=0, has_side_effects=True, vmem_limit_bytes=48 * 2**20
+        ),
+        name="exchange",
+    )(design_panel, design_front, weights, inverse_rows)
+    blk = blk.reshape((2 * groups, lines, size, piece))
+    tile = tile.reshape((2 * groups, halves, size, piece))
+    inv = inv.reshape((whole, inverse_rows.shape[1]))
+    return pl.pallas_call(
+        finish,
+        out_shape=(
+            jax.ShapeDtypeStruct((slab, cols), jnp.float32),
+            jax.ShapeDtypeStruct(front.shape, jnp.float32),
+        ),
+        in_specs=[pl.BlockSpec(memory_space=pltpu.SMEM)] + [vmem] * 4,
+        out_specs=(vmem, vmem),
+        scratch_shapes=[
+            pltpu.VMEM((lines, whole, piece), bf16),
+            pltpu.VMEM((halves, whole, piece), bf16),
+            pltpu.VMEM((halves, whole, piece), bf16),
+        ],
+        compiler_params=pltpu.CompilerParams(vmem_limit_bytes=48 * 2**20),
+        name="finish",
+    )(place.astype(jnp.int32)[None], blk, tile, inv, front)
+
+
 def solution(mesh):
     placed = (
         P("obs", ("team", "grid")),
@@ -58,8 +398,10 @@
         P(("team", "obs"), None),
         P(("team", "obs"), "grid"),
     )
+    sizes = mesh.shape
+    fits = sizes["team"] == 2 and sizes["obs"] == 4 and sizes["grid"] == 4
     return jax.shard_map(
-        local,
+        functools.partial(local_kernels, sizes["obs"]) if fits else local,
         mesh=mesh,
         in_specs=placed,
         out_specs=(P(("team", "obs"), "grid"), P(("team", "obs"), "grid")),

time: 279 us -> 135 us (0.48)
  the two profiles are of different devices: /device:TPU:20 before, /device:TPU:3 now
where the time goes in v2:
time: 135 us
  Pallas kernels  130 us (96%)
  other arithmetic  2.76 us (2%)
  between operations  1.41 us (1%)
    pallas_call x1, Pallas kernels, local_kernels(): pl.pallas_call(functools.partial(exchange, ratio), out_shape=(jax.ShapeDt...  111 us
    pallas_call x1, Pallas kernels, local_kernels(): pl.pallas_call(finish, out_shape=(jax.ShapeDtypeStruct((slab, cols), jnp....  19.3 us

profile of v2, /device:TPU:3, one launch (start us, length us, event | category | flops | bytes accessed | tf_op | source)
XLA Modules:
  0.0 134.9 jit_solution(13766489348415854013)
XLA Ops:
  0.6 0.0 copy-start
  1.4 1.3 select_reduce_fusion
  2.7 1.3 reduce-precision_convert_fusion
  4.0 0.1 broadcast_in_dim.32
  4.1 0.4 copy.10
  4.5 0.1 fusion.weights
  4.6 0.0 copy-done
  4.6 110.9 %exchange.1 = (bf16[2,2,4,256,384]{4,3,2,1,0:T(8,128)(2,1)}, bf16[2,2,2,256,384]{4,3,2,1,0:T(8,128)(2,1)S(1)}, bf16[2,4,128,1152]{3,2,1,0:T(8,128)(2,1)S(1)}) custom-call(bf16[2048,128]{1,0:T(8,128)(2,1)S(1)} %copy-done, bf16[2048,1536]{1,0:T(8,128)(2,1)} %front_cols.1, f32[2048,1]{1,0:T(8,128)S(1)} %fusion.weights, ...), custom_call_target="tpu_custom_call" | custom-call | tf_op jit(solution)/shard_map/exchange/pallas_call | solution.py:342
  115.6 19.3 %finish.1 = (f32[128,1536]{1,0:T(8,128)}, f32[768,1536]{1,0:T(8,128)}) custom-call(s32[1]{0:T(128)} %bitcast.spot, bf16[4,4,256,384]{3,2,1,0:T(8,128)(2,1)} %bitcast.9, bf16[4,2,256,384]{3,2,1,0:T(8,128)(2,1)S(1)} %bitcast.8, bf16[1024,1152]{1,0:T(8,128)(2,1)S(1)} %bitcast.7, f32[768,1536]{1,0:T(8,128)} %front.1), custom_call_target="tpu_custom_call" | custom-call | tf_op jit(solution)/shard_map/finish/pallas_call | solution.py:373
  (2 shorter events, 0.0 us)
Async XLA Ops:
  0.6 4.0 %copy-start = (bf16[2048,128]{1,0:T(8,128)(2,1)S(1)}, bf16[2048,128]{1,0:T(8,128)(2,1)}, u32[]{:S(2)}) copy-start(bf16[2048,128]{1,0:T(8,128)(2,1)} %panel.1) | copy-start | bytes 1572868

commit v3 on v2

--- a/solution.py
+++ b/solution.py
@@ -61,7 +61,7 @@
     panels, scaled, outgoing, incoming, own_sum,
     local_sem, panel_send, panel_recv, sum_send, sum_recv,
     line_send, line_recv, inv_send, inv_recv,
-    team_send, team_recv, team_inv_send, team_inv_recv, tile_send, tile_recv,
+    team_send, team_recv, inv_team_send, inv_team_recv, inv_grid_send, inv_grid_recv, tile_send, tile_recv,
 ):
     team, z, grid = lax.axis_index("team"), lax.axis_index("obs"), lax.axis_index("grid")
     lines = blk.shape[2]
@@ -100,14 +100,23 @@
         return panels.at[lax.div(index, 2), :, pl.ds(pl.multiple_of(lax.rem(index, 2) * width, width), width)]
 
     panel_copies = []
-    for k, peer in enumerate((beside_x, beside_y, across)):
+    for k, peer in enumerate((beside_x, beside_y)):
         panel_copies.append(
             remote(panel, panel_slot(grid), panel_send.at[k], panel_recv.at[k], {"grid": peer})
         )
         panel_copies[-1].start()
+    rows = panel.shape[0]
+    middle = rows // 2
+    for k, (source, peer) in enumerate(((beside_x, beside_y), (beside_y, beside_x))):
+        cut = panel_slot(source).at[pl.ds(k * middle, middle)]
+        panel_copies.append(
+            remote(cut, cut, panel_send.at[2 + k], panel_recv.at[2 + k], {"grid": peer})
+        )
     own_panel = pltpu.make_async_copy(panel, panel_slot(grid), local_sem.at[0])
     own_panel.start()
-    own_inv = pltpu.make_async_copy(inverse_rows, inv.at[team, z], local_sem.at[1])
+    share = inv.shape[3]
+    own_rows = inverse_rows.at[pl.ds(pl.multiple_of(grid * share, share), share)]
+    own_inv = pltpu.make_async_copy(own_rows, inv.at[team, z, grid], local_sem.at[1])
     own_inv.start()
 
     def line_sends(ref_of, send, recv, s):
@@ -142,17 +151,14 @@
                     pltpu.make_async_copy(ref_of(idx), ref_of(idx), send.at[d, s]).wait()
 
     def inv_of(idx):
-        return inv.at[team, idx]
-
-    def inv_to_team(idx):
-        remote(inv.at[team, idx], inv.at[team, idx], team_inv_send.at[idx],
-               team_inv_recv.at[idx], {"team": partner}).start()
+        return inv.at[team, idx, grid]
+
+    def nothing(idx):
+        pass
 
     own_inv.wait()
     line_sends(inv_of, inv_send, inv_recv, 0)
-    inv_to_team(z)
-
-    rows = panel.shape[0]
+
     step_rows = 256
 
     @pl.loop(0, rows // step_rows)
@@ -168,13 +174,16 @@
     for order in range(groups):
         g = y if order == 0 else 1 - y
         if order == 0:
+            for s in range(lines - 2):
+                line_waits(inv_of, inv_send, inv_recv, s, nothing)
+                line_sends(inv_of, inv_send, inv_recv, s + 1)
             panel_copies[0].wait_recv()
+            panel_copies[2].start()
+            panel_copies[1].wait_recv()
+            panel_copies[3].start()
         else:
-            panel_copies[1].wait_recv()
             panel_copies[2].wait_recv()
-            for s in range(lines - 2):
-                line_waits(inv_of, inv_send, inv_recv, s, inv_to_team)
-                line_sends(inv_of, inv_send, inv_recv, s + 1)
+            panel_copies[3].wait_recv()
         for p in (2, 1, 3, 0):
             dest = lax.rem(z + p, lines)
             total = contract_rows(panels[g], scaled[dest])
@@ -189,7 +198,12 @@
                 copy.start()
                 sum_copies.append(copy)
 
-    line_waits(inv_of, inv_send, inv_recv, lines - 2, inv_to_team)
+    line_waits(inv_of, inv_send, inv_recv, lines - 2, nothing)
+    inv_copies = []
+    for k, peer in enumerate((beside_x, beside_y, across)):
+        own = inv.at[team, :, grid]
+        inv_copies.append(remote(own, own, inv_grid_send.at[k], inv_grid_recv.at[k], {"grid": peer}))
+        inv_copies[-1].start()
 
     def finished(t, g, order, idx):
         @pl.when(is_root & (lax.div(idx, per_half) == half))
@@ -219,6 +233,38 @@
         line_sends(of, line_send.at[order], line_recv.at[order], 0)
         line_done(g, order, z)
 
+    def settle(idx):
+        for order in range(groups):
+            g = y if order == 0 else 1 - y
+            pltpu.make_async_copy(
+                blk.at[partner, g, idx], blk.at[partner, g, idx], team_recv.at[g, idx]
+            ).wait()
+            finished(partner, g, order, idx)
+
+    def relay(idx):
+        for t in (team, partner):
+            for order in range(groups):
+                g = y if order == 0 else 1 - y
+
+                @pl.when(is_relay & (lax.div(idx, per_half) == half))
+                def _():
+                    q = lax.rem(idx, per_half)
+                    dst = tile.at[t, g, q]
+                    pltpu.make_async_copy(dst, dst, tile_recv.at[t, g, q]).wait()
+                    remote(dst, dst, tile_send.at[0, t, g, q], tile_recv.at[t, g, q],
+                           {"grid": beside_y}).start()
+
+    def each_at(s, then):
+        if s < 0:
+            then(z)
+            return
+        for step in (1, -1):
+            came = z - step * (s + 1)
+
+            @pl.when((came >= 0) & (came < lines))
+            def _():
+                then(jnp.clip(came, 0, lines - 1))
+
     for s in range(lines - 1):
         for order in range(groups):
             g = y if order == 0 else 1 - y
@@ -230,38 +276,36 @@
                        lambda idx: line_done(g, order, idx))
             if s + 1 < lines - 1:
                 line_sends(of, line_send.at[order], line_recv.at[order], s + 1)
-
-    for order in range(groups):
-        g = y if order == 0 else 1 - y
-        for idx in range(lines):
-            pltpu.make_async_copy(
-                blk.at[partner, g, idx], blk.at[partner, g, idx], team_recv.at[g, idx]
-            ).wait()
-            finished(partner, g, order, idx)
+        if s == 0:
+            for copy in inv_copies:
+                copy.wait_recv()
+            inv_team = remote(inv.at[team], inv.at[team], inv_team_send, inv_team_recv, {"team": partner})
+            inv_team.start()
+        each_at(s - 1, settle)
+        if s > 0:
+            each_at(s - 2, relay)
+    each_at(lines - 2, settle)
+    each_at(lines - 3, relay)
+    each_at(lines - 2, relay)
 
     for t in (team, partner):
         for order in range(groups):
             g = y if order == 0 else 1 - y
             for q in range(per_half):
                 dst = tile.at[t, g, q]
-                pltpu.make_async_copy(dst, dst, tile_recv.at[t, g, q]).wait()
-
-                @pl.when(is_relay)
-                def _():
-                    remote(dst, dst, tile_send.at[0, t, g, q], tile_recv.at[t, g, q],
-                           {"grid": beside_y}).start()
-
-    for copy in panel_copies + sum_copies:
+
+                @pl.when(jnp.logical_not(is_relay))
+                def _():
+                    pltpu.make_async_copy(dst, dst, tile_recv.at[t, g, q]).wait()
+
+    inv_team.wait()
+    for copy in panel_copies + sum_copies + inv_copies:
         copy.wait_send()
     line_drain(inv_of, inv_send)
     for order in range(groups):
         g = y if order == 0 else 1 - y
         line_drain(lambda idx: blk.at[team, g, idx], line_send.at[order])
     for idx in range(lines):
-        ref = inv.at[team, idx]
-        pltpu.make_async_copy(ref, ref, team_inv_send.at[idx]).wait()
-        ref = inv.at[partner, idx]
-        pltpu.make_async_copy(ref, ref, team_inv_recv.at[idx]).wait()
         for g in range(groups):
             ref = blk.at[team, g, idx]
             pltpu.make_async_copy(ref, ref, team_send.at[g, idx]).wait()
@@ -316,7 +360,7 @@
             front_out[at] = front[at] - update
 
 
-def local_kernels(lines, design_panel, design_front, arc_ids, arc_weight, row_counts, panel_inverse, front):
+def local_kernels(lines, grids, design_panel, design_front, arc_ids, arc_weight, row_counts, panel_inverse, front):
     bf16 = jnp.bfloat16
     weights = live_weights(arc_ids, arc_weight, row_counts)[:, None]
     slab, whole = panel_inverse.shape
@@ -344,7 +388,7 @@
         out_shape=(
             jax.ShapeDtypeStruct((2, groups, lines, size, piece), bf16),
             jax.ShapeDtypeStruct((2, groups, halves, size, piece), bf16),
-            jax.ShapeDtypeStruct((2, lines) + inverse_rows.shape, bf16),
+            jax.ShapeDtypeStruct((2, lines, grids, slab // grids, inverse_rows.shape[1]), bf16),
         ),
         in_specs=[vmem] * 4,
         out_specs=(vmem,) * 3,
@@ -354,12 +398,12 @@
             pltpu.VMEM((groups, hops, size, piece), bf16),
             pltpu.VMEM((groups, hops, size, piece), bf16),
             pltpu.VMEM((groups, size, piece), jnp.float32),
-            dma((2,)), dma((3,)), dma((3,)),
+            dma((2,)), dma((4,)), dma((4,)),
             dma((groups, hops)), dma((groups, hops)),
             dma((groups, 2, hops)), dma((groups, 2, hops)),
             dma((2, hops)), dma((2, hops)),
             dma((groups, lines)), dma((groups, lines)),
-            dma((lines,)), dma((lines,)),
+            dma, dma, dma((3,)), dma((3,)),
             dma((2, 2, groups, halves)), dma((2, groups, halves)),
         ],
         compiler_params=pltpu.CompilerParams(
@@ -401,7 +445,7 @@
     sizes = mesh.shape
     fits = sizes["team"] == 2 and sizes["obs"] == 4 and sizes["grid"] == 4
     return jax.shard_map(
-        functools.partial(local_kernels, sizes["obs"]) if fits else local,
+        functools.partial(local_kernels, sizes["obs"], sizes["grid"]) if fits else local,
         mesh=mesh,
         in_specs=placed,
         out_specs=(P(("team", "obs"), "grid"), P(("team", "obs"), "grid")),

time: 135 us -> 119 us (0.88)
  the two profiles are of different devices: /device:TPU:3 before, /device:TPU:20 now
where the time goes in v3:
time: 119 us
  Pallas kernels  114 us (96%)
  other arithmetic  2.76 us (2%)
  between operations  1.41 us (1%)
    pallas_call x1, Pallas kernels, local_kernels(): pl.pallas_call(functools.partial(exchange, ratio), out_shape=(jax.ShapeDt...  94.8 us
    pallas_call x1, Pallas kernels, local_kernels(): pl.pallas_call(finish, out_shape=(jax.ShapeDtypeStruct((slab, cols), jnp....  19.3 us

profile of v3, /device:TPU:20, one launch (start us, length us, event | category | flops | bytes accessed | tf_op | source)
XLA Modules:
  0.0 118.7 jit_solution(3452939381119638724)
XLA Ops:
  0.6 0.0 copy-start
  1.4 1.3 %select_reduce_fusion = f32[2048]{0:T(1024)S(1)} fusion(f32[128]{0:T(128)} %param.10, s32[2048]{0:T(1024)} %param.9), kind=kLoop, calls=%fused_computation | loop fusion | flops 784384 | bytes 16896 | tf_op jit(solution)/shard_map/reduce_sum | solution.py:15
  2.7 1.3 %reduce-precision_convert_fusion = (bf16[128,1024]{1,0:T(8,128)(2,1)S(1)}, bf16[128]{0:T(256)(128)(2,1)S(1)}) fusion(f32[128,1024]{1,0:T(8,128)} %param.12, s32[128]{0:T(128)S(1)} %iota_add_fusion), kind=kLoop, calls=%fused_computation.5 | loop fusion | flops 786304 | bytes 787200 | tf_op jit(solution)/shard_map/convert
  4.0 0.1 broadcast_in_dim.32
  4.1 0.4 copy.10
  4.5 0.1 fusion.weights
  4.6 0.0 copy-done
  4.6 94.8 %exchange.1 = (bf16[2,2,4,256,384]{4,3,2,1,0:T(8,128)(2,1)}, bf16[2,2,2,256,384]{4,3,2,1,0:T(8,128)(2,1)S(1)}, bf16[2,4,4,32,1152]{4,3,2,1,0:T(8,128)(2,1)S(1)}) custom-call(bf16[2048,128]{1,0:T(8,128)(2,1)S(1)} %copy-done, bf16[2048,1536]{1,0:T(8,128)(2,1)} %front_cols.1, f32[2048,1]{1,0:T(8,128)S(1)} %fusion.weights, ...), custom_call_target="tpu_custom_call" | custom-call | tf_op jit(solution)/shard_map/exchange/pallas_call | solution.py:386
  99.4 19.3 %finish.1 = (f32[128,1536]{1,0:T(8,128)}, f32[768,1536]{1,0:T(8,128)}) custom-call(s32[1]{0:T(128)} %bitcast.spot, bf16[4,4,256,384]{3,2,1,0:T(8,128)(2,1)} %bitcast.9, bf16[4,2,256,384]{3,2,1,0:T(8,128)(2,1)S(1)} %bitcast.8, bf16[1024,1152]{1,0:T(8,128)(2,1)S(1)} %bitcast.7, f32[768,1536]{1,0:T(8,128)} %front.1), custom_call_target="tpu_custom_call" | custom-call | tf_op jit(solution)/shard_map/finish/pallas_call | solution.py:417
  (2 shorter events, 0.0 us)
Async XLA Ops:
  0.6 4.0 %copy-start = (bf16[2048,128]{1,0:T(8,128)(2,1)S(1)}, bf16[2048,128]{1,0:T(8,128)(2,1)}, u32[]{:S(2)}) copy-start(bf16[2048,128]{1,0:T(8,128)(2,1)} %panel.1) | copy-start | bytes 1572868

commit v4 on v3

--- a/solution.py
+++ b/solution.py
@@ -323,11 +323,14 @@
                     pltpu.make_async_copy(ref, ref, tile_send.at[1, t, g, q]).wait()
 
 
-def finish(spot, blk, tile, inv, front, factor_out, front_out, cols, high, low):
+def finish(spot, blk, tile, inv, front, factor_out, front_out, cols, high, low, held, sems):
     pieces, blocks, size = blk.shape[1], blk.shape[0], blk.shape[2]
     piece = blk.shape[3]
     whole = blocks * size
     slab = factor_out.shape[0]
+
+    load = pltpu.make_async_copy(front, held, sems.at[0])
+    load.start()
 
     def factor_of(source, q, r):
         total = inv[r * size:(r + 1) * size, whole:whole + 1].astype(jnp.float32)
@@ -349,15 +352,25 @@
                     factor_out[:, q * piece:(q + 1) * piece] = value[part * slab:(part + 1) * slab]
         for q in range(tile.shape[1]):
             value = factor_of(tile, q, r)
+            value = value.T
             top = value.astype(jnp.bfloat16)
-            high[q, r * size:(r + 1) * size, :] = top
-            low[q, r * size:(r + 1) * size, :] = (value - top.astype(jnp.float32)).astype(jnp.bfloat16)
-
+            high[q, :, r * size:(r + 1) * size] = top
+            low[q, :, r * size:(r + 1) * size] = (value - top.astype(jnp.float32)).astype(jnp.bfloat16)
+
+    load.wait()
+    stores = []
     for h in range(tile.shape[1]):
         for q in range(pieces):
-            update = contract_rows(high[h], cols[q]) + contract_rows(low[h], cols[q])
-            at = (slice(h * piece, (h + 1) * piece), slice(q * piece, (q + 1) * piece))
-            front_out[at] = front[at] - update
+            update = jnp.dot(high[h], cols[q], preferred_element_type=jnp.float32)
+            update += jnp.dot(low[h], cols[q], preferred_element_type=jnp.float32)
+            at = (pl.ds(h * piece, piece), pl.ds(q * piece, piece))
+            held[at] = held[at] - update
+            stores.append(
+                pltpu.make_async_copy(held.at[at], front_out.at[at], sems.at[1 + h * pieces + q])
+            )
+            stores[-1].start()
+    for store in stores:
+        store.wait()
 
 
 def local_kernels(lines, grids, design_panel, design_front, arc_ids, arc_weight, row_counts, panel_inverse, front):
@@ -420,12 +433,14 @@
             jax.ShapeDtypeStruct((slab, cols), jnp.float32),
             jax.ShapeDtypeStruct(front.shape, jnp.float32),
         ),
-        in_specs=[pl.BlockSpec(memory_space=pltpu.SMEM)] + [vmem] * 4,
-        out_specs=(vmem, vmem),
+        in_specs=[pl.BlockSpec(memory_space=pltpu.SMEM)] + [vmem] * 3 + [pl.BlockSpec(memory_space=pl.ANY)],
+        out_specs=(vmem, pl.BlockSpec(memory_space=pl.ANY)),
         scratch_shapes=[
             pltpu.VMEM((lines, whole, piece), bf16),
-            pltpu.VMEM((halves, whole, piece), bf16),
-            pltpu.VMEM((halves, whole, piece), bf16),
+            pltpu.VMEM((halves, piece, whole), bf16),
+            pltpu.VMEM((halves, piece, whole), bf16),
+            pltpu.VMEM(front.shape, jnp.float32),
+            dma((1 + halves * lines,)),
         ],
         compiler_params=pltpu.CompilerParams(vmem_limit_bytes=48 * 2**20),
         name="finish",

time: 119 us -> 118 us (level)
    pallas_call x1, Pallas kernels: 19.3 us -> 17.8 us  [local_kernels(): pl.pallas_call(finish, out_shape=(jax.ShapeDtypeStruct((slab, cols), jnp....]
where the time goes in v4:
time: 118 us; the launch traced here: 117 us
  Pallas kernels  113 us (96%)
  other arithmetic  2.76 us (2%)
  between operations  1.57 us (1%)
    pallas_call x1, Pallas kernels, local_kernels(): pl.pallas_call(functools.partial(exchange, ratio), out_shape=(jax.ShapeDt...  94.8 us
    pallas_call x1, Pallas kernels, local_kernels(): pl.pallas_call(finish, out_shape=(jax.ShapeDtypeStruct((slab, cols), jnp....  17.8 us

profile of v4, /device:TPU:20, one launch (start us, length us, event | category | flops | bytes accessed | tf_op | source)
XLA Modules:
  0.0 117.3 jit_solution(7710222256735348513)
XLA Ops:
  0.6 0.0 copy-start
  1.4 1.3 %select_reduce_fusion = f32[2048]{0:T(1024)S(1)} fusion(f32[128]{0:T(128)} %param.10, s32[2048]{0:T(1024)} %param.9), kind=kLoop, calls=%fused_computation | loop fusion | flops 784384 | bytes 16896 | tf_op jit(solution)/shard_map/reduce_sum | solution.py:15
  2.7 1.3 %reduce-precision_convert_fusion = (bf16[128,1024]{1,0:T(8,128)(2,1)S(1)}, bf16[128]{0:T(256)(128)(2,1)S(1)}) fusion(f32[128,1024]{1,0:T(8,128)} %param.12, s32[128]{0:T(128)S(1)} %iota_add_fusion), kind=kLoop, calls=%fused_computation.5 | loop fusion | flops 786304 | bytes 787200 | tf_op jit(solution)/shard_map/convert
  4.0 0.1 broadcast_in_dim.32
  4.1 0.4 copy.10
  4.5 0.1 fusion.weights
  4.6 0.0 copy-done
  4.6 94.8 %exchange.1 = (bf16[2,2,4,256,384]{4,3,2,1,0:T(8,128)(2,1)}, bf16[2,2,2,256,384]{4,3,2,1,0:T(8,128)(2,1)S(1)}, bf16[2,4,4,32,1152]{4,3,2,1,0:T(8,128)(2,1)S(1)}) custom-call(bf16[2048,128]{1,0:T(8,128)(2,1)S(1)} %copy-done, bf16[2048,1536]{1,0:T(8,128)(2,1)} %front_cols.1, f32[2048,1]{1,0:T(8,128)S(1)} %fusion.weights, ...), custom_call_target="tpu_custom_call" | custom-call | tf_op jit(solution)/shard_map/exchange/pallas_call | solution.py:399
  99.4 17.8 %finish.1 = (f32[128,1536]{1,0:T(8,128)}, f32[768,1536]{1,0:T(8,128)}) custom-call(s32[1]{0:T(128)} %bitcast.spot, bf16[4,4,256,384]{3,2,1,0:T(8,128)(2,1)} %bitcast.9, bf16[4,2,256,384]{3,2,1,0:T(8,128)(2,1)S(1)} %bitcast.8, bf16[1024,1152]{1,0:T(8,128)(2,1)S(1)} %bitcast.7, f32[768,1536]{1,0:T(8,128)} %front.1), custom_call_target="tpu_custom_call" | custom-call | tf_op jit(solution)/shard_map/finish/pallas_call | solution.py:430
  (2 shorter events, 0.0 us)
Async XLA Ops:
  0.6 4.0 %copy-start = (bf16[2048,128]{1,0:T(8,128)(2,1)S(1)}, bf16[2048,128]{1,0:T(8,128)(2,1)}, u32[]{:S(2)}) copy-start(bf16[2048,128]{1,0:T(8,128)(2,1)} %panel.1) | copy-start | bytes 1572868
